TPU v7x, 32 devices: a whole 2x2x4 slice. The times are simulated.
32 devices in a mesh: dp: 8 (over z, x), tensor: 4 (over y, core).
Axes of the slice: x: 2, y: 2, z: 4, core: 2. Of those that a mesh axis runs over, the one named last changes fastest.
Arguments:
- tokens: bfloat16 [16, 512, 768], P('dp'), may hold values from -6 to 6
- lengths: int32 [16], P('dp'), may hold values from 1 to 512, 2048 in all
- groups: int32 [16, 512], P('dp'), may hold values from 0 to 3, never falling along the last dimension, each value on 1 to 256 neighbouring positions
- key_mask: int32 [16, 512], P('dp'), may hold values 0 or 1
- w_query: bfloat16 [768, 768], P(None, 'tensor'), may hold values from -0.21875 to 0.21875
- b_query: float32 [768], P('tensor'), may hold values from -3 to 3
- w_key: bfloat16 [768, 768], P(None, 'tensor'), may hold values from -0.21875 to 0.21875
- w_value: bfloat16 [768, 768], P(None, 'tensor'), may hold values from -0.21875 to 0.21875
- b_value: float32 [768], P('tensor'), may hold values from -3 to 3
- rel_bias: float32 [12, 256], P('tensor'), may hold values from -4 to 4
- w_out: bfloat16 [768, 768], P('tensor'), may hold values from -0.625 to 0.625
- b_out: float32 [768], replicated, may hold values from -3 to 3
- gain_one: float32 [768], replicated, may hold values from 0.25 to 1.75
- shift_one: float32 [768], replicated, may hold values from -3 to 3
- w_inner: bfloat16 [768, 3072], P(None, 'tensor'), may hold values from -0.21875 to 0.21875
- b_inner: float32 [3072], P('tensor'), may hold values from -3 to 3
- w_outer: bfloat16 [3072, 768], P('tensor'), may hold values from -0.109375 to 0.109375
- b_outer: float32 [768], replicated, may hold values from -3 to 3
- gain_two: float32 [768], replicated, may hold values from 0.25 to 1.75
- shift_two: float32 [768], replicated, may hold values from -3 to 3
- cotangent: bfloat16 [16, 256, 768], P('dp'), may hold values from -24 to 24
Outputs:
- output: bfloat16 [16, 256, 768], P('dp')
- grad_tokens: bfloat16 [16, 512, 768], P('dp')
- grad_w_query: float32 [768, 768], P(None, 'tensor')
- grad_b_query: float32 [768], P('tensor')
- grad_w_key: float32 [768, 768], P(None, 'tensor')
- grad_w_value: float32 [768, 768], P(None, 'tensor')
- grad_b_value: float32 [768], P('tensor')
- grad_rel_bias: float32 [12, 256], P('tensor')
- grad_w_out: float32 [768, 768], P('tensor')
- grad_b_out: float32 [768], replicated
- grad_gain_one: float32 [768], replicated
- grad_shift_one: float32 [768], replicated
- grad_w_inner: float32 [768, 3072], P(None, 'tensor')
- grad_b_inner: float32 [3072], P('tensor')
- grad_w_outer: float32 [3072, 768], P('tensor')
- grad_b_outer: float32 [768], replicated
- grad_gain_two: float32 [768], replicated
- grad_shift_two: float32 [768], replicated
Inputs may be any that keep to these rules, and one draw needn't show every extreme that they name: `lengths`: the longest row has exactly 512 used tokens. `groups`: document ids never fall along a row; a document has at most half of 512 positions.
All inputs are finite; a program needn't handle non-finite values. No bound on the sum of `lengths` or of `key_mask` on one device may be relied on, other than what follows from the above.
Results may differ from a plain program's by a relative error of at most 0.013.
Values sent between devices are 32-bit elements; how exact they have to be, the bound alone decides.
No kernel may reach another device: no remote copies, remote signals or barrier semaphores. Data moves between devices by JAX's collectives and lax.ppermute only.
A program may use at most 128 MiB of HBM per device.

v0:
```python
import jax
import jax.numpy as jnp
from jax import lax
from jax.sharding import PartitionSpec as P


def diagonal_table(seq, width):
    span = 2 * seq
    offset = jnp.arange(span, dtype=jnp.int32)
    distance = jnp.where(offset < seq, offset, offset - span)
    bucket = jnp.clip(distance, -(width // 2), width // 2 - 1) + width // 2
    return (bucket[:, None] == jnp.arange(width, dtype=jnp.int32)[None, :]).astype(jnp.float32)


def skewed_bias(rel_bias, onehot, half, seq):
    heads = rel_bias.shape[0]
    span = 2 * seq
    line = jnp.dot(rel_bias, onehot.T, precision=lax.Precision.HIGHEST)
    tiled = jnp.tile(line, (1, half))[:, : half * (span - 2)]
    return tiled.reshape(heads, half, span - 2)[:, :, :seq]


def skewed_bias_grad(score_sum, onehot, half, seq):
    heads = score_sum.shape[0]
    span = 2 * seq
    padded = jnp.pad(score_sum, ((0, 0), (0, 0), (0, span - 2 - seq))).reshape(
        heads, half * (span - 2)
    )
    padded = jnp.pad(padded, ((0, 0), (0, 2 * half))).reshape(heads, half, span)
    along = jnp.sum(padded, axis=1)
    return jnp.dot(along, onehot, precision=lax.Precision.HIGHEST)


def allowed_keys(lengths, groups, key_mask):
    seq = groups.shape[1]
    keyed = jnp.arange(seq, dtype=jnp.int32)
    own = groups[:, 0::2]
    same = own[:, :, None] == groups[:, None, :]
    live = (keyed[None, :] < lengths[:, None]) & (key_mask == 1)
    self_key = keyed[None, :] == 2 * jnp.arange(seq // 2, dtype=jnp.int32)[:, None]
    return same & live[:, None, :] | self_key[None]


def norm_forward(value, gain, shift):
    centre = value - jnp.mean(value, axis=-1, keepdims=True)
    spread = jnp.mean(centre * centre, axis=-1, keepdims=True)
    factor = lax.rsqrt(spread + 1e-05)
    normed = centre * factor
    return (normed * gain + shift, normed, factor)


def norm_backward(grad_out, normed, factor, gain):
    grad_norm = grad_out * gain
    first_mean = jnp.mean(grad_norm, axis=-1, keepdims=True)
    second_mean = jnp.mean(grad_norm * normed, axis=-1, keepdims=True)
    grad_in = factor * (grad_norm - first_mean - normed * second_mean)
    return (grad_in, jnp.sum(grad_out * normed, axis=(0, 1)), jnp.sum(grad_out, axis=(0, 1)))


def project(left, right):
    return jnp.einsum("rld,de->rle", left, right, preferred_element_type=jnp.float32)


def project_back(left, right):
    return jnp.einsum("rle,de->rld", left, right, preferred_element_type=jnp.float32)


def weight_grad(left, right):
    return jnp.einsum("rld,rle->de", left, right, preferred_element_type=jnp.float32)


def exact_gelu(value):
    return jax.nn.gelu(value, approximate=False)


def local(
    tokens,
    lengths,
    groups,
    key_mask,
    w_query,
    b_query,
    w_key,
    w_value,
    b_value,
    rel_bias,
    w_out,
    b_out,
    gain_one,
    shift_one,
    w_inner,
    b_inner,
    w_outer,
    b_outer,
    gain_two,
    shift_two,
    cotangent,
):
    rows, seq, width = tokens.shape
    half = seq // 2
    heads, table = rel_bias.shape
    head_dim = w_query.shape[1] // heads
    wide = tokens.astype(jnp.float32)
    pooled = jnp.sum(wide.reshape(rows, half, 2, width), axis=2) * 0.5
    pooled_low = pooled.astype(jnp.bfloat16)
    query = (project(pooled_low, w_query) + b_query).astype(jnp.bfloat16)
    keys = project(tokens, w_key).astype(jnp.bfloat16)
    values = (project(tokens, w_value) + b_value).astype(jnp.bfloat16)
    query_heads = query.reshape(rows, half, heads, head_dim)
    key_heads = keys.reshape(rows, seq, heads, head_dim)
    value_heads = values.reshape(rows, seq, heads, head_dim)
    onehot = diagonal_table(seq, table)
    bias = skewed_bias(rel_bias, onehot, half, seq)
    allowed = allowed_keys(lengths, groups, key_mask)[:, None]

    def masked_scores():
        raw = (
            jnp.einsum(
                "rqhe,rkhe->rhqk", query_heads, key_heads, preferred_element_type=jnp.float32
            )
            * 0.125
            + bias[None]
        )
        return jnp.where(allowed, raw, -1e30)

    scores = masked_scores()
    top = jnp.max(scores, axis=-1, keepdims=True)
    expo = jnp.exp(scores - top)
    total = jnp.sum(expo, axis=-1, keepdims=True)
    log_total = top + jnp.log(total)
    prob_low = (expo / total).astype(jnp.bfloat16)
    context = jnp.einsum(
        "rhqk,rkhe->rqhe", prob_low, value_heads, preferred_element_type=jnp.float32
    )
    context = context.astype(jnp.bfloat16).reshape(rows, half, heads * head_dim)
    attn = lax.psum(project(context, w_out), "tensor")
    first = pooled + (attn + b_out)
    y_one, normed_one, factor_one = norm_forward(first, gain_one, shift_one)
    y_low = y_one.astype(jnp.bfloat16)
    inner = project(y_low, w_inner) + b_inner
    act = exact_gelu(inner).astype(jnp.bfloat16)
    ffn = lax.psum(project(act, w_outer), "tensor")
    second = y_one + (ffn + b_outer)
    result, normed_two, factor_two = norm_forward(second, gain_two, shift_two)
    output = result.astype(jnp.bfloat16)
    grad_out = cotangent.astype(jnp.float32)
    grad_second, grad_gain_two, grad_shift_two = norm_backward(
        grad_out, normed_two, factor_two, gain_two
    )
    grad_b_outer = jnp.sum(grad_second, axis=(0, 1))
    grad_ffn = grad_second.astype(jnp.bfloat16)
    grad_w_outer = weight_grad(act, grad_ffn)
    grad_act = project_back(grad_ffn, w_outer)
    gelu_pull = jax.vjp(exact_gelu, inner)[1]
    grad_inner = gelu_pull(grad_act)[0].astype(jnp.bfloat16)
    grad_b_inner = jnp.sum(grad_inner.astype(jnp.float32), axis=(0, 1))
    grad_w_inner = weight_grad(y_low, grad_inner)
    grad_y = grad_second + lax.psum(project_back(grad_inner, w_inner), "tensor")
    grad_first, grad_gain_one, grad_shift_one = norm_backward(
        grad_y, normed_one, factor_one, gain_one
    )
    grad_b_out = jnp.sum(grad_first, axis=(0, 1))
    grad_attn = grad_first.astype(jnp.bfloat16)
    grad_w_out = weight_grad(context, grad_attn)
    grad_context = (
        project_back(grad_attn, w_out).astype(jnp.bfloat16).reshape(rows, half, heads, head_dim)
    )
    prob = jnp.exp(masked_scores() - log_total)
    grad_prob = jnp.einsum(
        "rqhe,rkhe->rhqk", grad_context, value_heads, preferred_element_type=jnp.float32
    )
    centre_term = jnp.sum(prob * grad_prob, axis=-1, keepdims=True)
    grad_scores = (prob * (grad_prob - centre_term)).astype(jnp.bfloat16)
    score_sum = jnp.sum(grad_scores.astype(jnp.float32), axis=0)
    grad_rel_bias = skewed_bias_grad(score_sum, onehot, half, seq)
    grad_query = (
        jnp.einsum("rhqk,rkhe->rqhe", grad_scores, key_heads, preferred_element_type=jnp.float32)
        * 0.125
    ).astype(jnp.bfloat16)
    grad_keys = (
        jnp.einsum("rhqk,rqhe->rkhe", grad_scores, query_heads, preferred_element_type=jnp.float32)
        * 0.125
    ).astype(jnp.bfloat16)
    grad_values = jnp.einsum(
        "rhqk,rqhe->rkhe", prob_low, grad_context, preferred_element_type=jnp.float32
    ).astype(jnp.bfloat16)
    grad_query = grad_query.reshape(rows, half, heads * head_dim)
    grad_keys = grad_keys.reshape(rows, seq, heads * head_dim)
    grad_values = grad_values.reshape(rows, seq, heads * head_dim)
    grad_b_query = jnp.sum(grad_query.astype(jnp.float32), axis=(0, 1))
    grad_b_value = jnp.sum(grad_values.astype(jnp.float32), axis=(0, 1))
    grad_w_query = weight_grad(pooled_low, grad_query)
    grad_w_key = weight_grad(tokens, grad_keys)
    grad_w_value = weight_grad(tokens, grad_values)
    pooled_part = project_back(grad_query, w_query)
    token_part = project_back(grad_keys, w_key) + project_back(grad_values, w_value)
    pooled_sum, token_sum = lax.psum((pooled_part, token_part), "tensor")
    grad_pooled = grad_first + pooled_sum
    grad_tokens = (token_sum + jnp.repeat(grad_pooled * 0.5, 2, axis=1)).astype(jnp.bfloat16)
    (
        grad_w_query,
        grad_b_query,
        grad_w_key,
        grad_w_value,
        grad_b_value,
        grad_rel_bias,
        grad_w_out,
        grad_b_out,
        grad_gain_one,
        grad_shift_one,
        grad_w_inner,
        grad_b_inner,
        grad_w_outer,
        grad_b_outer,
        grad_gain_two,
        grad_shift_two,
    ) = lax.psum(
        (
            grad_w_query,
            grad_b_query,
            grad_w_key,
            grad_w_value,
            grad_b_value,
            grad_rel_bias,
            grad_w_out,
            grad_b_out,
            grad_gain_one,
            grad_shift_one,
            grad_w_inner,
            grad_b_inner,
            grad_w_outer,
            grad_b_outer,
            grad_gain_two,
            grad_shift_two,
        ),
        "dp",
    )
    return (
        output,
        grad_tokens,
        grad_w_query,
        grad_b_query,
        grad_w_key,
        grad_w_value,
        grad_b_value,
        grad_rel_bias,
        grad_w_out,
        grad_b_out,
        grad_gain_one,
        grad_shift_one,
        grad_w_inner,
        grad_b_inner,
        grad_w_outer,
        grad_b_outer,
        grad_gain_two,
        grad_shift_two,
    )


def solution(mesh):
    placed = (
        P("dp", None, None),
        P("dp"),
        P("dp", None),
        P("dp", None),
        P(None, "tensor"),
        P("tensor"),
        P(None, "tensor"),
        P(None, "tensor"),
        P("tensor"),
        P("tensor", None),
        P("tensor", None),
        P(),
        P(),
        P(),
        P(None, "tensor"),
        P("tensor"),
        P("tensor", None),
        P(),
        P(),
        P(),
        P("dp", None, None),
    )
    return jax.shard_map(
        local,
        mesh=mesh,
        in_specs=placed,
        out_specs=(
            P("dp", None, None),
            P("dp", None, None),
            P(None, "tensor"),
            P("tensor"),
            P(None, "tensor"),
            P(None, "tensor"),
            P("tensor"),
            P("tensor", None),
            P("tensor", None),
            P(),
            P(),
            P(),
            P(None, "tensor"),
            P("tensor"),
            P("tensor", None),
            P(),
            P(),
            P(),
        ),
        check_vma=False,
    )
```

profile of v0, /device:TPU:0, one launch (start us, length us, event | category | flops | bytes accessed | tf_op | source)
XLA Modules:
  0.0 569.8 jit_solution(7469340155090265146)
XLA Ops:
  9.1 5.0 reshape.201
  15.8 2.2 copy.45
  18.0 2.8 slice.12
  20.8 7.5 %reshape.191 = f32[3,256,1022]{2,1,0:T(8,128)} reshape(f32[3,261632]{1,0:T(4,128)} %slice.12) | data formatting | bytes 6279168 | tf_op jit(solution)/shard_map/reshape | solution.py:20
  29.1 5.6 reduce_sum.202
  44.7 45.5 %all-reduce.11.cloned.1.call-done = f32[2,256,768]{2,1,0:T(8,128)} async-done(((f32[2,256,768]{2,1,0:T(8,128)}), f32[2,256,768]{2,1,0:T(8,128)}) %all-reduce.11.cloned.1.call-update) | async-done | bytes 1572880 | tf_op jit(solution)/shard_map/psum | solution.py:136
  90.2 2.2 fusion.59
  94.3 4.5 multiply_convert_fusion.1
  99.6 1.9 fusion.18
  101.6 43.0 %all-reduce.13.cloned.1.call-done = f32[2,256,768]{2,1,0:T(8,128)} async-done(((f32[2,256,768]{2,1,0:T(8,128)}), f32[2,256,768]{2,1,0:T(8,128)}) %all-reduce.13.cloned.1.call-update) | async-done | bytes 1572880 | tf_op jit(solution)/shard_map/psum | solution.py:142
  144.7 2.0 fusion.57
  149.4 2.2 convert_reduce_fusion.2
  152.5 2.0 fusion.20
  155.3 42.4 %all-reduce.15.cloned.1.call-done = f32[2,256,768]{2,1,0:T(8,128)} async-done(((f32[2,256,768]{2,1,0:T(8,128)}), f32[2,256,768]{2,1,0:T(8,128)}) %all-reduce.15.cloned.1.call-update) | async-done | bytes 1572880 | tf_op jit(solution)/shard_map/psum | solution.py:158
  197.7 4.6 fusion.8
  207.1 2.2 convert_reduce_fusion
  211.5 1.6 fusion.40
  214.0 2.4 convolution_add_fusion
  217.2 3.7 convolution_bitcast_fusion.1
  220.9 2.5 convolution_bitcast_fusion
  230.1 3.6 pad.8
  233.7 7.6 %reshape.198 = f32[3,261632]{1,0:T(4,128)} reshape(f32[3,256,1022]{2,1,0:T(8,128)} %pad.8) | data formatting | bytes 6279168 | tf_op jit(solution)/shard_map/reshape | solution.py:26
  241.3 2.7 pad.9
  244.1 1.7 bitcast_reduce_fusion
  246.3 38.5 %all-reduce.2 = (f32[192]{0:T(256)}, f32[192]{0:T(256)}, f32[3,256]{1,0:T(4,128)}, f32[768]{0:T(1024)}, f32[768]{0:T(1024)}, /*index=5*/f32[768]{0:T(1024)}, f32...) all-reduce(f32[192]{0:T(256)S(1)} %reduce_sum.214, ...), channel_id=1, replica_groups=mesh['dp'=8,'tensor'=4] {'dp'}, use_global_device_ids=true, to_apply=%region_19.20 | all-reduce | flops 6528 | bytes 52224 | tf_op jit(solution)/shard_map/psum | solution.py:217
  284.8 26.1 %all-reduce.19.cloned.1.call-done = (f32[2,512,768]{2,1,0:T(8,128)}, f32[2,256,768]{2,1,0:T(8,128)}) async-done(((f32[2,512,768]{2,1,0:T(8,128)}, f32[2,256,768]{2,1,0:T(8,128)}), (f32[2,512,768]{2,1,0:T(8,128)}, f32[2,256,768]{2,1,0:T(8,128)})) %all-reduce.19.cloned.1.call-update) | async-done | bytes 4718608 | tf_op jit(solution)/shard_map/psum | solution.py:197
  310.8 1.6 add_multiply_fusion
  312.5 2.8 broadcast_in_dim.16
  315.3 5.3 reshape.197
  320.6 5.1 add_convert_fusion
  325.6 228.9 %all-reduce.17.cloned.1.call-done = (f32[768,192]{0,1:T(8,128)}, f32[768,192]{0,1:T(8,128)}, f32[768,192]{0,1:T(8,128)}, f32[192,768]{1,0:T(8,128)}, f32[768,768]{1,0:T(8,128)}, /*index=5*/f32[768,768]{1,0:T(8,128)}) async-done(((f32[768,192]{0,1:T(8,128)}, f32[768,192]{0,1:T(8,128)}, f32[768,192]{0,1:T(8,128)}, f32[192,768]{1,0:T(8,128)}, f32[768,768]{1,0:T(8,128)}, /*index=5*/f32[768,768]{1,0:T(8,128)}), ...) | async-done | bytes 7077904 | tf_op jit(solution)/shard_map/psum | solution.py:217
  554.5 2.0 copy.59
  (243 shorter events, 43.4 us)
Async XLA Ops:
  7.2 85.5 %copy-start = (bf16[768,768]{1,0:T(8,128)(2,1)S(1)}, bf16[768,768]{1,0:T(8,128)(2,1)}, u32[]{:S(2)}) copy-start(bf16[768,768]{1,0:T(8,128)(2,1)} %param.35) | copy-start | bytes 3538948
  7.2 83.0 %all-reduce.11.cloned.1.call-start = ((), (), s32[]{:S(2)}) async-start(), calls=%async_computation | async-start | bytes 3145728 | tf_op jit(solution)/shard_map/psum | solution.py:136
  7.3 7.5 %copy-start.78 = (s32[1024]{0:T(1024)}, s32[1024]{0:T(1024)S(1)}, u32[]{:S(2)}) copy-start(s32[1024]{0:T(1024)S(1)} %fusion.48) | copy-start | bytes 12292
  9.1 5.0 copy-start.10
  9.1 5.0 copy-start.38
  14.8 21.9 %copy-start.25 = (bf16[2,512,192]{1,2,0:T(8,128)(2,1)}, bf16[2,512,192]{1,2,0:T(8,128)(2,1)S(1)}, u32[]{:S(2)}) copy-start(bf16[2,512,192]{1,2,0:T(8,128)(2,1)S(1)} %convolution_convert_fusion.1) | copy-start | bytes 1179652
  29.1 5.7 copy-start.66
  29.1 7.1 %copy-start.29 = (bf16[768,192]{0,1:T(8,128)(2,1)S(1)}, bf16[768,192]{0,1:T(8,128)(2,1)}, u32[]{:S(2)}) copy-start(bf16[768,192]{0,1:T(8,128)(2,1)} %param.25) | copy-start | bytes 884740
  29.1 7.2 %copy-start.84 = (f32[192]{0:T(256)S(1)}, f32[192]{0:T(256)}, u32[]{:S(2)}) copy-start(f32[192]{0:T(256)} %param.26) | copy-start | bytes 2308
  42.9 47.3 %copy-start.75 = (f32[768]{0:T(1024)S(1)}, f32[768]{0:T(1024)}, u32[]{:S(2)}) copy-start(f32[768]{0:T(1024)} %param.32) | copy-start | bytes 9220
  44.5 100.2 %all-reduce.13.cloned.1.call-start = ((), (), s32[]{:S(2)}) async-start(), calls=%async_computation.1 | async-start | bytes 3145728 | tf_op jit(solution)/shard_map/psum | solution.py:142
  92.4 52.3 %copy-start.43 = (f32[2,256]{1,0:T(2,128)}, f32[2,256]{1,0:T(2,128)S(1)}, u32[]{:S(2)}) copy-start(f32[2,256]{1,0:T(2,128)S(1)} %broadcast_multiply_fusion.5) | copy-start | bytes 6148
  93.1 51.6 %copy-start.49 = (f32[2,256]{1,0:T(2,128)}, f32[2,256]{1,0:T(2,128)S(1)}, u32[]{:S(2)}) copy-start(f32[2,256]{1,0:T(2,128)S(1)} %add_rsqrt_fusion.1) | copy-start | bytes 6148
  94.3 4.5 copy-start.22
  94.3 5.4 copy-start.86
  101.6 43.1 %copy-start.81 = (f32[768]{0:T(1024)S(1)}, f32[768]{0:T(1024)}, u32[]{:S(2)}) copy-start(f32[768]{0:T(1024)} %param.38) | copy-start | bytes 9220
  101.6 96.1 %all-reduce.15.cloned.1.call-start = ((), (), s32[]{:S(2)}) async-start(), calls=%async_computation.2 | async-start | bytes 3145728 | tf_op jit(solution)/shard_map/psum | solution.py:158
  144.7 4.4 copy-start.87
  154.5 43.2 %copy-start.44 = (f32[2,256]{1,0:T(2,128)S(1)}, f32[2,256]{1,0:T(2,128)}, u32[]{:S(2)}) copy-start(f32[2,256]{1,0:T(2,128)} %copy-done.43) | copy-start | bytes 6148
  154.5 43.2 %copy-start.47 = (f32[768]{0:T(1024)S(1)}, f32[768]{0:T(1024)}, u32[]{:S(2)}) copy-start(f32[768]{0:T(1024)} %param.33) | copy-start | bytes 9220
  154.5 43.2 %copy-start.50 = (f32[2,256]{1,0:T(2,128)S(1)}, f32[2,256]{1,0:T(2,128)}, u32[]{:S(2)}) copy-start(f32[2,256]{1,0:T(2,128)} %copy-done.49) | copy-start | bytes 6148
  154.5 43.2 %copy-start.53 = (f32[2,256]{1,0:T(2,128)S(1)}, f32[2,256]{1,0:T(2,128)}, u32[]{:S(2)}) copy-start(f32[2,256]{1,0:T(2,128)} %copy-done.52) | copy-start | bytes 6148
  154.5 43.2 %copy-start.56 = (f32[2,256]{1,0:T(2,128)S(1)}, f32[2,256]{1,0:T(2,128)}, u32[]{:S(2)}) copy-start(f32[2,256]{1,0:T(2,128)} %copy-done.55) | copy-start | bytes 6148
  154.5 43.2 %copy-start.59 = (f32[768]{0:T(1024)S(1)}, f32[768]{0:T(1024)}, u32[]{:S(2)}) copy-start(f32[768]{0:T(1024)} %param.39) | copy-start | bytes 9220
  154.5 43.2 %copy-start.70 = (f32[2,256]{1,0:T(2,128)S(1)}, f32[2,256]{1,0:T(2,128)}, u32[]{:S(2)}) copy-start(f32[2,256]{1,0:T(2,128)} %copy-done.69) | copy-start | bytes 6148
  154.6 43.2 %copy-start.73 = (f32[2,256]{1,0:T(2,128)S(1)}, f32[2,256]{1,0:T(2,128)}, u32[]{:S(2)}) copy-start(f32[2,256]{1,0:T(2,128)} %copy-done.72) | copy-start | bytes 6148
  154.6 43.2 %copy-start.76 = (f32[768]{0:T(1024)S(1)}, f32[768]{0:T(1024)}, u32[]{:S(2)}) copy-start(f32[768]{0:T(1024)} %param.40) | copy-start | bytes 9220
  154.6 156.2 %all-reduce.19.cloned.1.call-start = ((), (), s32[]{:S(2)}) async-start(), calls=%async_computation.4 | async-start | bytes 9437184 | tf_op jit(solution)/shard_map/psum | solution.py:197
  216.4 4.4 copy-start.54
  216.5 4.4 copy-start.57
  216.5 4.4 copy-start.60
  216.5 338.0 %all-reduce.17.cloned.1.call-start = ((), (), s32[]{:S(2)}) async-start(), calls=%async_computation.3 | async-start | bytes 14155776 | tf_op jit(solution)/shard_map/psum | solution.py:217
  (66 other events, 121.9 us)
Sparse Core Ops, SparseCore 0:
  44.6 45.5 all-reduce.10
  101.7 42.8 all-reduce.12
  154.7 42.8 all-reduce.14
  216.6 94.2 all-reduce.18
  316.9 237.5 all-reduce.16
where the time goes:
time: 575 us; the launch traced here: 570 us
  waiting for transfers between devices  386 us (67%)
  local copies, waits for them, and re-layouts  60.4 us (11%)
  blocking collectives  38.5 us (7%)
  other arithmetic  36.3 us (6%)
  matrix products  33.2 us (6%)
  between operations  14.9 us (3%)
    psum x1, waiting for transfers between devices, local(): lax.psum((grad_w_query, grad_b_query, grad_w_key, grad_w_value, grad_b_va...  229 us
    psum x1, waiting for transfers between devices, local(): attn = lax.psum(project(context, w_out), 'tensor')  45.5 us
    psum x1, waiting for transfers between devices, local(): ffn = lax.psum(project(act, w_outer), 'tensor')  43 us
    psum x1, waiting for transfers between devices, local(): grad_y = grad_second + lax.psum(project_back(grad_inner, w_inner), 'tensor')  42.4 us
    psum x1, blocking collectives, local(): lax.psum((grad_w_query, grad_b_query, grad_w_key, grad_w_value, grad_b_va...  38.5 us
    psum x1, waiting for transfers between devices, local(): pooled_sum, token_sum = lax.psum((pooled_part, token_part), 'tensor')  26.1 us
    unnamed x192, local copies, waits for them, and re-layouts  21.8 us
  transfers between devices with their start and end apart: 5, of which 5 were waited for; matrix products, arithmetic and copies ran while one was open for 7% of the time, Pallas kernels for 0%

commit v1 on v0

--- a/solution.py
+++ b/solution.py
@@ -133,7 +133,8 @@
         "rhqk,rkhe->rqhe", prob_low, value_heads, preferred_element_type=jnp.float32
     )
     context = context.astype(jnp.bfloat16).reshape(rows, half, heads * head_dim)
-    attn = lax.psum(project(context, w_out), "tensor")
+    xs = project(context, w_out)
+    attn = jnp.sum(jax.lax.all_gather(xs, "tensor"), 0)
     first = pooled + (attn + b_out)
     y_one, normed_one, factor_one = norm_forward(first, gain_one, shift_one)
     y_low = y_one.astype(jnp.bfloat16)

time: 575 us -> 583 us (1.014)
    all_gather x0 -> x1, waiting for transfers between devices: none -> 49 us  [local(): attn = jnp.sum(jax.lax.all_gather(xs, 'tensor'), 0)]
    psum x1 -> x0, waiting for transfers between devices: 45.5 us -> none  [local(): attn = lax.psum(project(context, w_out), 'tensor')]
where the time goes in v1:
time: 583 us; the launch traced here: 578 us
  waiting for transfers between devices  389 us (67%)
  local copies, waits for them, and re-layouts  60.4 us (10%)
  other arithmetic  40.8 us (7%)
  blocking collectives  38.5 us (7%)
  matrix products  33.2 us (6%)
  between operations  14.9 us (3%)
    psum x1, waiting for transfers between devices, local(): lax.psum((grad_w_query, grad_b_query, grad_w_key, grad_w_value, grad_b_va...  229 us
    all_gather x1, waiting for transfers between devices, local(): attn = jnp.sum(jax.lax.all_gather(xs, 'tensor'), 0)  49 us
    psum x1, waiting for transfers between devices, local(): ffn = lax.psum(project(act, w_outer), 'tensor')  43 us
    psum x1, waiting for transfers between devices, local(): grad_y = grad_second + lax.psum(project_back(grad_inner, w_inner), 'tensor')  42.4 us
    psum x1, blocking collectives, local(): lax.psum((grad_w_query, grad_b_query, grad_w_key, grad_w_value, grad_b_va...  38.5 us
    psum x1, waiting for transfers between devices, local(): pooled_sum, token_sum = lax.psum((pooled_part, token_part), 'tensor')  26.1 us
    unnamed x192, local copies, waits for them, and re-layouts  21.9 us
  transfers between devices with their start and end apart: 5, of which 5 were waited for; matrix products, arithmetic and copies ran while one was open for 7% of the time, Pallas kernels for 0%

profile of v1, /device:TPU:0, one launch (start us, length us, event | category | flops | bytes accessed | tf_op | source)
XLA Modules:
  0.0 577.8 jit_solution(13805171496610927688)
XLA Ops:
  9.1 5.0 reshape.201
  15.8 2.2 copy.47
  18.0 2.8 slice.12
  20.8 7.5 %reshape.191 = f32[3,256,1022]{2,1,0:T(8,128)} reshape(f32[3,261632]{1,0:T(4,128)} %slice.12) | data formatting | bytes 6279168 | tf_op jit(solution)/shard_map/reshape | solution.py:20
  29.1 5.6 reduce_sum.211
  44.8 49.0 %all-gather.3.cloned.1.call-done = f32[8,256,768]{2,1,0:T(8,128)} async-done(((f32[2,256,768]{2,1,0:T(8,128)}), f32[8,256,768]{2,1,0:T(8,128)}) %all-gather.3.cloned.1.call-update) | async-done | bytes 6291472 | tf_op jit(solution)/shard_map/all_gather | solution.py:137
  93.8 4.5 reduce_sum.213
  98.3 2.2 fusion.59
  102.4 4.5 multiply_convert_fusion.1
  107.8 1.9 fusion.18
  109.8 43.0 %all-reduce.10.cloned.1.call-done = f32[2,256,768]{2,1,0:T(8,128)} async-done(((f32[2,256,768]{2,1,0:T(8,128)}), f32[2,256,768]{2,1,0:T(8,128)}) %all-reduce.10.cloned.1.call-update) | async-done | bytes 1572880 | tf_op jit(solution)/shard_map/psum | solution.py:143
  152.7 2.0 fusion.57
  157.5 2.2 convert_reduce_fusion.2
  160.6 2.0 fusion.20
  163.3 42.4 %all-reduce.12.cloned.1.call-done = f32[2,256,768]{2,1,0:T(8,128)} async-done(((f32[2,256,768]{2,1,0:T(8,128)}), f32[2,256,768]{2,1,0:T(8,128)}) %all-reduce.12.cloned.1.call-update) | async-done | bytes 1572880 | tf_op jit(solution)/shard_map/psum | solution.py:159
  205.8 4.6 fusion.8
  215.2 2.2 convert_reduce_fusion
  222.1 2.4 convolution_add_fusion
  225.2 3.7 convolution_bitcast_fusion.1
  229.0 2.5 convolution_bitcast_fusion
  238.2 3.6 pad.8
  241.8 7.6 %reshape.198 = f32[3,261632]{1,0:T(4,128)} reshape(f32[3,256,1022]{2,1,0:T(8,128)} %pad.8) | data formatting | bytes 6279168 | tf_op jit(solution)/shard_map/reshape | solution.py:26
  249.4 2.7 pad.9
  252.1 1.7 bitcast_reduce_fusion
  254.3 38.5 %all-reduce.2 = (f32[192]{0:T(256)}, f32[192]{0:T(256)}, f32[3,256]{1,0:T(4,128)}, f32[768]{0:T(1024)}, f32[768]{0:T(1024)}, /*index=5*/f32[768]{0:T(1024)}, f32...) all-reduce(f32[192]{0:T(256)S(1)} %reduce_sum.224, ...), channel_id=1, replica_groups=mesh['dp'=8,'tensor'=4] {'dp'}, use_global_device_ids=true, to_apply=%region_19.20 | all-reduce | flops 6528 | bytes 52224 | tf_op jit(solution)/shard_map/psum | solution.py:218
  292.8 26.1 %all-reduce.16.cloned.1.call-done = (f32[2,512,768]{2,1,0:T(8,128)}, f32[2,256,768]{2,1,0:T(8,128)}) async-done(((f32[2,512,768]{2,1,0:T(8,128)}, f32[2,256,768]{2,1,0:T(8,128)}), (f32[2,512,768]{2,1,0:T(8,128)}, f32[2,256,768]{2,1,0:T(8,128)})) %all-reduce.16.cloned.1.call-update) | async-done | bytes 4718608 | tf_op jit(solution)/shard_map/psum | solution.py:198
  318.9 1.6 add_multiply_fusion
  320.5 2.8 broadcast_in_dim.16
  323.4 5.3 reshape.197
  328.6 5.1 add_convert_fusion
  333.7 228.9 %all-reduce.14.cloned.1.call-done = (f32[768,192]{0,1:T(8,128)}, f32[768,192]{0,1:T(8,128)}, f32[768,192]{0,1:T(8,128)}, f32[192,768]{1,0:T(8,128)}, f32[768,768]{1,0:T(8,128)}, /*index=5*/f32[768,768]{1,0:T(8,128)}) async-done(((f32[768,192]{0,1:T(8,128)}, f32[768,192]{0,1:T(8,128)}, f32[768,192]{0,1:T(8,128)}, f32[192,768]{1,0:T(8,128)}, f32[768,768]{1,0:T(8,128)}, /*index=5*/f32[768,768]{1,0:T(8,128)}), ...) | async-done | bytes 7077904 | tf_op jit(solution)/shard_map/psum | solution.py:218
  562.6 2.0 copy.60
  (244 shorter events, 45.0 us)
Async XLA Ops:
  7.2 93.7 %copy-start = (bf16[768,768]{1,0:T(8,128)(2,1)S(1)}, bf16[768,768]{1,0:T(8,128)(2,1)}, u32[]{:S(2)}) copy-start(bf16[768,768]{1,0:T(8,128)(2,1)} %param.35) | copy-start | bytes 3538948
  7.2 86.6 %all-gather.3.cloned.1.call-start = ((), (), s32[]{:S(2)}) async-start(), calls=%async_computation.2 | async-start | bytes 7864320 | tf_op jit(solution)/shard_map/all_gather | solution.py:137
  7.3 7.5 %copy-start.78 = (s32[1024]{0:T(1024)}, s32[1024]{0:T(1024)S(1)}, u32[]{:S(2)}) copy-start(s32[1024]{0:T(1024)S(1)} %fusion.48) | copy-start | bytes 12292
  9.1 5.0 copy-start.10
  9.1 5.0 copy-start.38
  14.8 21.9 %copy-start.25 = (bf16[2,512,192]{1,2,0:T(8,128)(2,1)}, bf16[2,512,192]{1,2,0:T(8,128)(2,1)S(1)}, u32[]{:S(2)}) copy-start(bf16[2,512,192]{1,2,0:T(8,128)(2,1)S(1)} %convolution_convert_fusion.1) | copy-start | bytes 1179652
  29.1 5.7 copy-start.66
  29.1 7.1 %copy-start.29 = (bf16[768,192]{0,1:T(8,128)(2,1)S(1)}, bf16[768,192]{0,1:T(8,128)(2,1)}, u32[]{:S(2)}) copy-start(bf16[768,192]{0,1:T(8,128)(2,1)} %param.25) | copy-start | bytes 884740
  29.1 7.2 %copy-start.84 = (f32[192]{0:T(256)S(1)}, f32[192]{0:T(256)}, u32[]{:S(2)}) copy-start(f32[192]{0:T(256)} %param.26) | copy-start | bytes 2308
  44.6 108.2 %all-reduce.10.cloned.1.call-start = ((), (), s32[]{:S(2)}) async-start(), calls=%async_computation | async-start | bytes 3145728 | tf_op jit(solution)/shard_map/psum | solution.py:143
  93.8 4.5 copy-start.75
  100.5 52.2 %copy-start.43 = (f32[2,256]{1,0:T(2,128)}, f32[2,256]{1,0:T(2,128)S(1)}, u32[]{:S(2)}) copy-start(f32[2,256]{1,0:T(2,128)S(1)} %broadcast_multiply_fusion.5) | copy-start | bytes 6148
  101.2 51.5 %copy-start.49 = (f32[2,256]{1,0:T(2,128)}, f32[2,256]{1,0:T(2,128)S(1)}, u32[]{:S(2)}) copy-start(f32[2,256]{1,0:T(2,128)S(1)} %add_rsqrt_fusion.1) | copy-start | bytes 6148
  102.4 4.5 copy-start.22
  102.4 5.3 copy-start.86
  109.7 43.0 %copy-start.81 = (f32[768]{0:T(1024)S(1)}, f32[768]{0:T(1024)}, u32[]{:S(2)}) copy-start(f32[768]{0:T(1024)} %param.38) | copy-start | bytes 9220
  109.7 96.0 %all-reduce.12.cloned.1.call-start = ((), (), s32[]{:S(2)}) async-start(), calls=%async_computation.1 | async-start | bytes 3145728 | tf_op jit(solution)/shard_map/psum | solution.py:159
  152.7 4.4 copy-start.87
  162.6 43.2 %copy-start.44 = (f32[2,256]{1,0:T(2,128)S(1)}, f32[2,256]{1,0:T(2,128)}, u32[]{:S(2)}) copy-start(f32[2,256]{1,0:T(2,128)} %copy-done.43) | copy-start | bytes 6148
  162.6 43.2 %copy-start.47 = (f32[768]{0:T(1024)S(1)}, f32[768]{0:T(1024)}, u32[]{:S(2)}) copy-start(f32[768]{0:T(1024)} %param.33) | copy-start | bytes 9220
  162.6 43.2 %copy-start.50 = (f32[2,256]{1,0:T(2,128)S(1)}, f32[2,256]{1,0:T(2,128)}, u32[]{:S(2)}) copy-start(f32[2,256]{1,0:T(2,128)} %copy-done.49) | copy-start | bytes 6148
  162.6 43.2 %copy-start.53 = (f32[2,256]{1,0:T(2,128)S(1)}, f32[2,256]{1,0:T(2,128)}, u32[]{:S(2)}) copy-start(f32[2,256]{1,0:T(2,128)} %copy-done.52) | copy-start | bytes 6148
  162.6 43.2 %copy-start.56 = (f32[2,256]{1,0:T(2,128)S(1)}, f32[2,256]{1,0:T(2,128)}, u32[]{:S(2)}) copy-start(f32[2,256]{1,0:T(2,128)} %copy-done.55) | copy-start | bytes 6148
  162.6 43.2 %copy-start.59 = (f32[768]{0:T(1024)S(1)}, f32[768]{0:T(1024)}, u32[]{:S(2)}) copy-start(f32[768]{0:T(1024)} %param.39) | copy-start | bytes 9220
  162.6 43.2 %copy-start.70 = (f32[2,256]{1,0:T(2,128)S(1)}, f32[2,256]{1,0:T(2,128)}, u32[]{:S(2)}) copy-start(f32[2,256]{1,0:T(2,128)} %copy-done.69) | copy-start | bytes 6148
  162.6 43.2 %copy-start.73 = (f32[2,256]{1,0:T(2,128)S(1)}, f32[2,256]{1,0:T(2,128)}, u32[]{:S(2)}) copy-start(f32[2,256]{1,0:T(2,128)} %copy-done.72) | copy-start | bytes 6148
  162.6 43.2 %copy-start.76 = (f32[768]{0:T(1024)S(1)}, f32[768]{0:T(1024)}, u32[]{:S(2)}) copy-start(f32[768]{0:T(1024)} %param.40) | copy-start | bytes 9220
  162.7 156.3 %all-reduce.16.cloned.1.call-start = ((), (), s32[]{:S(2)}) async-start(), calls=%async_computation.4 | async-start | bytes 9437184 | tf_op jit(solution)/shard_map/psum | solution.py:198
  224.5 4.4 copy-start.54
  224.5 4.4 copy-start.57
  224.5 4.4 copy-start.60
  224.5 338.1 %all-reduce.14.cloned.1.call-start = ((), (), s32[]{:S(2)}) async-start(), calls=%async_computation.3 | async-start | bytes 14155776 | tf_op jit(solution)/shard_map/psum | solution.py:218
  (66 other events, 121.9 us)
Sparse Core Ops, SparseCore 0:
  44.7 49.0 all-gather.2
  109.8 42.8 all-reduce.9
  162.8 42.8 all-reduce.11
  224.6 94.2 all-reduce.15
  325.0 237.5 all-reduce.13
